TPU v7x, 32 devices: a whole 2x2x4 slice. The times are simulated.
32 devices in a mesh: grid: 4 (over y, x), comp: 8 (over z, core).
Axes of the slice: x: 2, y: 2, z: 4, core: 2. Of those that a mesh axis runs over, the one named last changes fastest.
Arguments:
- spectrum: bfloat16 [4, 1152, 4096], P('grid', 'comp'), may hold values from -6 to 6
- sea_mask: int32 [4, 4096], P('grid'), may hold values 0 or 1
- speed: float32 [4, 32], P('grid'), may hold values from 0.05 to 0.95
- coupling_a: bfloat16 [1152, 1152], replicated, may hold values from -0.1875 to 0.1875
- coupling_b: bfloat16 [1152, 1152], replicated, may hold values from -0.1875 to 0.1875
- send_index: int32 [4, 8, 4, 16], P('grid', 'comp'), may hold values from 0 to 511
- recv_index: int32 [4, 8, 64], P('grid', 'comp'), may hold values from 0 to 511
- recv_weight: float32 [4, 8, 64], P('grid', 'comp'), may hold values from 0.3 to 3
Outputs:
- final_spectrum: bfloat16 [4, 1152, 4096], P('grid', 'comp')
All inputs are finite; a program needn't handle non-finite values. No bound on the sum of `sea_mask` on one device may be relied on, other than what follows from the above.
Results may differ from a plain program's by a relative error of at most 0.0067.
Values may be sent and summed in bfloat16 or wider, within the bound.
A program may use at most 64 MiB of HBM per device.

v0:
```python
import math

import jax
import jax.numpy as jnp
from jax import lax
from jax.sharding import PartitionSpec as P

ND = 36
NF = 32
LX = 128
STEPS = 2


def padded_2(array, sides, width):
    for axis, dim in sides:
        peers, length = (lax.axis_size(axis), array.shape[dim])
        up = [(i, (i + 1) % peers) for i in range(peers - 1)]
        down = [(j, i) for i, j in up]
        last = lax.slice_in_dim(array, length - width, length, axis=dim)
        initial = lax.slice_in_dim(array, 0, width, axis=dim)
        before = lax.ppermute(last, axis, up)
        after = lax.ppermute(initial, axis, down)
        array = jnp.concatenate([before, array, after], axis=dim)
    return array


def courant(comp_index, speed_row):
    direction = comp_index // NF
    frequency = comp_index % NF
    heading = 2.0 * math.pi * direction.astype(jnp.float32) / ND
    onehot_table = (frequency[:, None] == jnp.arange(NF, dtype=jnp.int32)[None, :]).astype(
        jnp.float32
    )
    celerity = jnp.sum(onehot_table * speed_row[None, :], axis=1)
    return (celerity * jnp.cos(heading), celerity * jnp.sin(heading))


def sweep_columns(values, number):
    padded = jnp.pad(values, ((0, 0), (0, 0), (1, 1)))
    forward = padded[:, :, 2:]
    behind = padded[:, :, :-2]
    return (
        values
        - 0.5 * number * (forward - behind)
        + 0.5 * number * number * (forward - 2.0 * values + behind)
    )


def sweep_rows(values, number):
    padded = jnp.pad(values, ((0, 0), (1, 1), (0, 0)))
    forward = padded[:, 2:, :]
    behind = padded[:, :-2, :]
    return (
        values
        - 0.5 * number * (forward - behind)
        + 0.5 * number * number * (forward - 2.0 * values + behind)
    )


def propagate(spectra, sea_float, courant_x, courant_y):
    count = spectra.shape[0]
    values = spectra.astype(jnp.float32).reshape(count, -1, LX)
    land_sea = sea_float.reshape(1, -1, LX)
    values = sweep_columns(values, courant_x[:, None, None]) * land_sea
    values = sweep_rows(values, courant_y[:, None, None]) * land_sea
    return values.reshape(count, -1).astype(jnp.bfloat16)


def advect_block(points, sea_rows, courant_x, courant_y):
    count = points.shape[0]
    values = points.reshape(count, -1, LX)
    extended = padded_2(values, (("comp", 1),), 1)
    widened = extended.astype(jnp.float32)
    widened = sweep_columns(widened, courant_x[:, None, None]) * sea_rows[None]
    widened = sweep_rows(widened, courant_y[:, None, None]) * sea_rows[None]
    return widened[:, 1:-1, :].reshape(count, -1).astype(jnp.bfloat16)


def source(points, sea_part, coupling_a, coupling_b):
    first_term = jnp.dot(coupling_a, points, preferred_element_type=jnp.float32)
    second = jnp.dot(coupling_b, points, preferred_element_type=jnp.float32)
    return (
        points.astype(jnp.float32) + 0.5 * sea_part[None, :] * first_term * jnp.tanh(second)
    ).astype(jnp.bfloat16)


def average(updated, received, targets, weights):
    count = updated.shape[1]
    hits = targets[:, None] == jnp.arange(count, dtype=jnp.int32)[None, :]
    weighted = (received.astype(jnp.float32) * weights[:, None]).astype(jnp.bfloat16)
    onehot_table = hits.astype(jnp.bfloat16)
    gathered_sum = lax.dot_general(
        weighted, onehot_table, (((0,), (0,)), ((), ())), preferred_element_type=jnp.float32
    )
    numerator = updated.astype(jnp.float32) + gathered_sum
    denominator = 1.0 + jnp.sum(hits.astype(jnp.float32) * weights[:, None], axis=0)
    return (numerator / denominator[None, :]).astype(jnp.bfloat16)


def share_intersection(updated, targets, groups, total_comps, my_grid):
    outgoing = jnp.take(updated, targets, axis=1).T.reshape(groups, -1, total_comps)
    everything = lax.all_gather(outgoing, "grid", axis=0, tiled=True)
    received = lax.dynamic_index_in_dim(
        everything.reshape(groups, groups, -1, total_comps), my_grid, 1, keepdims=False
    )
    return received.reshape(-1, total_comps)


def local(spectrum, sea_mask, speed, coupling_a, coupling_b, send_index, recv_index, recv_weight):
    local_comps = spectrum.shape[1]
    columns = spectrum.shape[2]
    groups = lax.axis_size("grid")
    pieces = lax.axis_size("comp")
    block_len = columns // pieces
    total_comps = coupling_a.shape[0]
    comp_index = lax.axis_index("comp") * local_comps + jnp.arange(local_comps, dtype=jnp.int32)
    courant_x, courant_y = courant(comp_index, speed[0])
    sea_float = sea_mask[0].astype(jnp.float32)
    sea_part = lax.dynamic_slice_in_dim(sea_float, lax.axis_index("comp") * block_len, block_len)
    targets = send_index.reshape(-1)
    my_grid = lax.axis_index("grid")
    spectra = spectrum[0]
    full_x, full_y = courant(jnp.arange(total_comps, dtype=jnp.int32), speed[0])
    block_rows = block_len // LX
    padded_sea = jnp.pad(sea_float.reshape(-1, LX), ((1, 1), (0, 0)))
    sea_rows = lax.dynamic_slice_in_dim(
        padded_sea, lax.axis_index("comp") * block_rows, block_rows + 2, 0
    )
    advected = propagate(spectra, sea_float, courant_x, courant_y)
    points = lax.all_to_all(advected, "comp", split_axis=1, concat_axis=0, tiled=True)
    for turn_index in range(STEPS):
        if turn_index > 0:
            points = advect_block(points, sea_rows, full_x, full_y)
        updated = source(points, sea_part, coupling_a, coupling_b)
        received = share_intersection(updated, targets, groups, total_comps, my_grid)
        points = average(updated, received, recv_index[0, 0], recv_weight[0, 0])
    spectra = lax.all_to_all(points, "comp", split_axis=0, concat_axis=1, tiled=True)
    return spectra[None]


def solution(mesh):
    return jax.shard_map(
        local,
        mesh=mesh,
        in_specs=(
            P("grid", "comp", None),
            P("grid", None),
            P("grid", None),
            P(),
            P(),
            P("grid", "comp", None, None),
            P("grid", "comp", None),
            P("grid", "comp", None),
        ),
        out_specs=P("grid", "comp", None),
        check_vma=False,
    )
```

profile of v0, /device:TPU:0, one launch (start us, length us, event | category | flops | bytes accessed | tf_op | source)
XLA Modules:
  0.0 146.6 jit_solution(15378040489614585774)
XLA Ops:
  0.0 0.0 copy-start
  0.0 0.9 select_reduce_fusion.2
  0.9 0.1 broadcast_multiply_fusion.1
  1.0 0.7 convert_element_type.128
  1.7 1.5 %convert_bitcast_fusion = f32[18,8,32,128]{3,1,2,0:T(8,128)S(1)} fusion(bf16[1,144,4096]{2,1,0:T(8,128)(2,1)} %param.10), kind=kLoop, calls=%fused_computation.36 | loop fusion | flops 589824 | bytes 3538944
  3.2 0.4 copy.31
  3.6 1.8 %add_multiply_fusion.1 = f32[144,32,128]{2,1,0:T(8,128)S(1)} fusion(f32[144,32,128]{2,1,0:T(8,128)S(1)} %bitcast.50, f32[32,128]{1,0:T(8,128)S(1)} %bitcast.61, f32[144]{0:T(256)S(1)} %get-tuple-element.18, f32[144]{0:T(256)S(1)} %get-tuple-element.19), kind=kLoop, calls=%fused_computation.38 | loop fusion | flops 5308416 | bytes 4736128 | tf_op jit(solution)/shard_map/mul | solution.py:64
  5.5 2.3 %multiply_convert_fusion = bf16[144,32,128]{2,1,0:T(8,128)(2,1)} fusion(f32[144,32,128]{2,1,0:T(8,128)S(1)} %add_multiply_fusion.1, f32[144]{0:T(256)S(1)} %get-tuple-element.17, f32[144]{0:T(256)S(1)} %get-tuple-element.16, f32[32,128]{1,0:T(8,128)S(1)} %bitcast.62), kind=kLoop, calls=%fused_computation.37 | loop fusion | flops 5898240 | bytes 3556480 | tf_op jit(solution)/shard_map/convert_element_type | solution.py:66
  7.7 3.2 %convert_element_type.131 = bf16[144,8,512]{2,1,0:T(8,128)(2,1)} reshape(bf16[144,32,128]{2,1,0:T(8,128)(2,1)} %multiply_convert_fusion) | data formatting | bytes 2359296 | tf_op jit(solution)/shard_map/convert_element_type | solution.py:66
  10.9 2.7 %copy.25 = bf16[144,8,512]{2,0,1:T(8,128)(2,1)} copy(bf16[144,8,512]{2,1,0:T(8,128)(2,1)} %convert_element_type.131) | data formatting | bytes 2359296 | tf_op jit(solution)/shard_map/convert_element_type | solution.py:66
  13.6 6.4 %all-to-all-start = ((bf16[144,8,512]{2,0,1:T(8,128)(2,1)}), bf16[144,8,512]{2,0,1:T(8,128)(2,1)}, u32[]{:S(2)}, u32[]{:S(2)}) async-start(bf16[144,8,512]{2,0,1:T(8,128)(2,1)} %copy.25), calls=%async_computation | async-start | bytes 2359296 | tf_op jit(solution)/shard_map/all_to_all | solution.py:130
  19.9 0.0 copy-done.3
  19.9 0.1 reshape.180
  20.1 0.0 copy-done.4
  20.1 0.0 copy-done.5
  20.1 0.1 select_reduce_fusion.1
  20.3 29.2 %all-to-all-done = bf16[144,8,512]{2,0,1:T(8,128)(2,1)} async-done(((bf16[144,8,512]{2,0,1:T(8,128)(2,1)}), bf16[144,8,512]{2,0,1:T(8,128)(2,1)}, u32[]{:S(2)}, u32[]{:S(2)}) %all-to-all-start) | async-done | bytes 1179680 | tf_op jit(solution)/shard_map/all_to_all | solution.py:130
  49.4 2.4 %copy.26 = bf16[1152,512]{0,1:T(8,128)(2,1)} copy(bf16[1152,512]{1,0:T(8,128)(2,1)} %bitcast.3) | data formatting | bytes 2359296 | tf_op jit(solution)/shard_map/all_to_all | solution.py:130
  51.8 0.0 copy-done
  51.8 3.3 %convolution_tanh_fusion.1 = f32[512,1152]{1,0:T(8,128)S(1)} fusion(bf16[1152,512]{1,0:T(8,128)(2,1)} %bitcast.3, bf16[1152,1152]{1,0:T(8,128)(2,1)S(1)} %copy-done), kind=kOutput, calls=%fused_computation.22 | convolution fusion | flops 1358954496 | bytes 6193152 | tf_op jit(solution)/shard_map/dot_general | solution.py:81
  55.1 0.0 copy-done.1
  55.1 4.3 %fusion.11 = bf16[1152,512]{0,1:T(8,128)(2,1)} fusion(f32[512,1152]{1,0:T(8,128)S(1)} %convolution_tanh_fusion.1, bf16[1152,512]{1,0:T(8,128)(2,1)} %bitcast.3, bf16[1152,1152]{1,0:T(8,128)(2,1)S(1)} %copy-done.6, bf16[1152,512]{0,1:T(8,128)(2,1)S(1)} %copy-done.1, f32[512]{0:T(512)S(1)} %bitcast.68), kind=kOutput, calls=%fused_computation.28 | convolution fusion | flops 1361903616 | bytes 8554496 | tf_op jit(solution)/shard_map/dot_general | solution.py:80
  59.4 2.3 %gather_fusion = bf16[64,1152]{1,0:T(8,128)(2,1)S(1)} fusion(bf16[1152,512]{0,1:T(8,128)(2,1)} %fusion.11, s32[1024]{0:T(1024)S(1)} %pad_clamp_fusion), kind=kCustom, calls=%fused_computation.clone | custom fusion | bytes 295168 | tf_op jit(solution)/shard_map/jit(_take)/gather | solution.py:101
  61.7 0.1 broadcast_select_fusion.1
  61.8 10.3 %all_gather.6 = bf16[16,16,1152]{2,1,0:T(8,128)(2,1)S(1)} all-gather(bf16[4,16,1152]{2,1,0:T(8,128)(2,1)S(1)} %bitcast.60), channel_id=1, replica_groups=mesh['grid'=4,'comp'=8] {'grid'}, dimensions={0}, use_global_device_ids=true | all-gather | bytes 737280 | tf_op jit(solution)/shard_map/all_gather | solution.py:102
  72.1 0.0 copy-start.2
  72.1 1.9 %fusion.9 = bf16[1152,512]{0,1:T(8,128)(2,1)S(1)} fusion(bf16[1152,512]{0,1:T(8,128)(2,1)} %fusion.11, f32[512]{0:T(512)S(1)} %broadcast_add_fusion, bf16[64,1152]{1,0:T(8,128)(2,1)S(1)} %bitcast.65, f32[64]{0:T(128)S(1)} %bitcast.71, s32[64]{0:T(128)S(1)} %bitcast.74), kind=kOutput, calls=%fused_computation.26 | convolution fusion | flops 78110720 | bytes 2509312 | tf_op jit(solution)/shard_map/dot_general | solution.py:92
  74.0 1.3 collective-permute-start
  75.4 1.5 %collective-permute-start.1 = (bf16[1152,1,128]{0,2,1:T(8,128)(2,1)S(1)}, bf16[1152,1,128]{0,2,1:T(8,128)(2,1)S(1)}, u32[]{:S(2)}, u32[]{:S(2)}) collective-permute-start(bf16[1152,1,128]{0,2,1:T(8,128)(2,1)S(1)} %get-tuple-element.11), channel_id=1, source_target_pairs={{1,0},{2,1},{3,2},{4,3},{5,4},{6,5},{7,6},{9,8},{10,9},{11,10},{12... | collective-permute-start | bytes 884744 | tf_op jit(solution)/shard_map/ppermute | solution.py:22
  76.9 0.1 select_reduce_fusion
  76.9 0.1 fusion.37
  77.0 0.0 collective-permute-done
  77.0 1.8 %collective-permute-done.1 = bf16[1152,1,128]{0,2,1:T(8,128)(2,1)S(1)} collective-permute-done((bf16[1152,1,128]{0,2,1:T(8,128)(2,1)S(1)}, bf16[1152,1,128]{0,2,1:T(8,128)(2,1)S(1)}, u32[]{:S(2)}, u32[]{:S(2)}) %collective-permute-start.1) | collective-permute-done | bytes 294944 | tf_op jit(solution)/shard_map/ppermute | solution.py:22
  78.8 0.3 maximum_convert_fusion
  79.1 1.7 %broadcast_multiply_fusion = (f32[1152,6,128]{0,2,1:T(8,128)S(1)}, f32[1152,6,128]{0,2,1:T(8,128)S(1)}) fusion(f32[6,128]{1,0:T(8,128)S(1)} %pad_dynamic-slice_fusion, f32[1152,6,128]{0,2,1:T(8,128)S(1)} %maximum_convert_fusion, f32[1152]{0:T(1024)S(1)} %get-tuple-element.13, f32[1152]{0:T(1024)S(1)} %get-tuple-element.15), kind=kLoop, calls=%fused_computation.40 | loop fusion | flops 8847360 | bytes 10629120 | tf_op jit(solution)/shard_map/mul | solution.py:56
  80.8 0.5 pad_slice_fusion.3
  81.3 0.7 fusion.14
  82.0 0.0 copy-start.7
  82.0 1.9 %convolution_tanh_fusion = f32[512,1152]{1,0:T(8,128)S(1)} fusion(bf16[1152,512]{0,1:T(8,128)(2,1)S(1)} %bitcast.55, bf16[1152,1152]{1,0:T(8,128)(2,1)S(1)} %copy-done), kind=kOutput, calls=%fused_computation.21 | convolution fusion | flops 1358954496 | bytes 6193152 | tf_op jit(solution)/shard_map/dot_general | solution.py:81
  84.0 3.0 %fusion.10 = bf16[1152,512]{0,1:T(8,128)(2,1)} fusion(f32[512,1152]{1,0:T(8,128)S(1)} %convolution_tanh_fusion, bf16[1152,512]{0,1:T(8,128)(2,1)S(1)} %bitcast.56, bf16[1152,1152]{1,0:T(8,128)(2,1)S(1)} %copy-done.7, f32[512]{0:T(512)S(1)} %bitcast.69), kind=kOutput, calls=%fused_computation.27 | convolution fusion | flops 1361903616 | bytes 7374848 | tf_op jit(solution)/shard_map/dot_general | solution.py:80
  87.0 2.3 %gather_fusion.1 = bf16[64,1152]{1,0:T(8,128)(2,1)S(1)} fusion(bf16[1152,512]{0,1:T(8,128)(2,1)} %fusion.10, s32[1024]{0:T(1024)S(1)} %pad_clamp_fusion), kind=kCustom, calls=%fused_computation.1.clone | custom fusion | bytes 295168 | tf_op jit(solution)/shard_map/jit(_take)/gather | solution.py:101
  89.2 0.1 broadcast_select_fusion
  89.3 10.5 %all_gather.7 = bf16[16,16,1152]{2,1,0:T(8,128)(2,1)S(1)} all-gather(bf16[4,16,1152]{2,1,0:T(8,128)(2,1)S(1)} %bitcast.59), channel_id=1, replica_groups=mesh['grid'=4,'comp'=8] {'grid'}, dimensions={0}, use_global_device_ids=true | all-gather | bytes 737280 | tf_op jit(solution)/shard_map/all_gather | solution.py:102
  99.9 2.9 %fusion.8 = bf16[1152,512]{0,1:T(8,128)(2,1)} fusion(bf16[1152,512]{0,1:T(8,128)(2,1)} %fusion.10, f32[512]{0:T(512)S(1)} %broadcast_add_fusion, bf16[64,1152]{1,0:T(8,128)(2,1)S(1)} %bitcast.64, f32[64]{0:T(128)S(1)} %bitcast.72, s32[64]{0:T(128)S(1)} %bitcast.75), kind=kOutput, calls=%fused_computation.25 | convolution fusion | flops 78110720 | bytes 2509312 | tf_op jit(solution)/shard_map/dot_general | solution.py:92
  102.8 2.4 %copy.28 = bf16[1152,512]{1,0:T(8,128)(2,1)} copy(bf16[1152,512]{0,1:T(8,128)(2,1)} %fusion.8) | data formatting | bytes 2359296 | tf_op jit(solution)/shard_map/convert_element_type | solution.py:97
  105.2 36.7 %all_to_all.32 = bf16[8,144,512]{2,1,0:T(8,128)(2,1)S(1)} all-to-all(bf16[8,144,512]{2,1,0:T(8,128)(2,1)} %bitcast.51), channel_id=1, replica_groups=mesh['grid'=4,'comp'=8] {'comp'}, dimensions={0} | all-to-all | bytes 2359296 | tf_op jit(solution)/shard_map/all_to_all | solution.py:137
  141.9 1.7 %copy.29 = bf16[144,8,512]{2,1,0:T(8,128)(2,1)} copy(bf16[144,8,512]{2,0,1:T(8,128)(2,1)S(1)} %bitcast.52) | data formatting | bytes 2359296 | tf_op jit(solution)/shard_map/all_to_all | solution.py:137
  143.6 3.1 %broadcast_in_dim.8 = bf16[1,144,4096]{2,1,0:T(8,128)(2,1)} reshape(bf16[144,8,512]{2,1,0:T(8,128)(2,1)} %copy.29) | data formatting | bytes 2359296 | tf_op jit(solution)/shard_map/broadcast_in_dim | solution.py:138
  (20 shorter events, 0.1 us)
Async XLA Ops:
  0.0 51.8 %copy-start = (bf16[1152,1152]{1,0:T(8,128)(2,1)S(1)}, bf16[1152,1152]{1,0:T(8,128)(2,1)}, u32[]{:S(2)}) copy-start(bf16[1152,1152]{1,0:T(8,128)(2,1)} %param.14) | copy-start | bytes 7962628
  10.9 9.0 %copy-start.3 = (s32[1,1,4,16]{3,2,1,0:T(4,128)S(1)}, s32[1,1,4,16]{3,2,1,0:T(4,128)}, u32[]{:S(2)}) copy-start(s32[1,1,4,16]{3,2,1,0:T(4,128)} %param.15) | copy-start | bytes 772
  10.9 9.2 %copy-start.4 = (f32[1,1,64]{2,1,0:T(1,128)S(1)}, f32[1,1,64]{2,1,0:T(1,128)}, u32[]{:S(2)}) copy-start(f32[1,1,64]{2,1,0:T(1,128)} %param.17) | copy-start | bytes 772
  10.9 9.2 %copy-start.5 = (s32[1,1,64]{2,1,0:T(1,128)S(1)}, s32[1,1,64]{2,1,0:T(1,128)}, u32[]{:S(2)}) copy-start(s32[1,1,64]{2,1,0:T(1,128)} %param.16) | copy-start | bytes 772
  13.6 35.8 %all-to-all-start = ((bf16[144,8,512]{2,0,1:T(8,128)(2,1)}), bf16[144,8,512]{2,0,1:T(8,128)(2,1)}, u32[]{:S(2)}, u32[]{:S(2)}) async-start(bf16[144,8,512]{2,0,1:T(8,128)(2,1)} %copy.25), calls=%async_computation | async-start | bytes 2359296 | tf_op jit(solution)/shard_map/all_to_all | solution.py:130
  51.8 3.3 %copy-start.1 = (bf16[1152,512]{0,1:T(8,128)(2,1)S(1)}, bf16[1152,512]{0,1:T(8,128)(2,1)}, u32[]{:S(2)}) copy-start(bf16[1152,512]{0,1:T(8,128)(2,1)} %copy.26) | copy-start | bytes 3538948
  51.8 3.3 %copy-start.6 = (bf16[1152,1152]{1,0:T(8,128)(2,1)S(1)}, bf16[1152,1152]{1,0:T(8,128)(2,1)}, u32[]{:S(2)}) copy-start(bf16[1152,1152]{1,0:T(8,128)(2,1)} %param.13) | copy-start | bytes 7962628
  72.1 4.8 %copy-start.2 = (f32[1,32]{1,0:T(1,128)S(1)}, f32[1,32]{1,0:T(1,128)}, u32[]{:S(2)}) copy-start(f32[1,32]{1,0:T(1,128)} %param.12) | copy-start | bytes 388
  74.0 3.0 %collective-permute-start = (bf16[1152,1,128]{0,2,1:T(8,128)(2,1)S(1)}, bf16[1152,1,128]{0,2,1:T(8,128)(2,1)S(1)}, u32[]{:S(2)}, u32[]{:S(2)}) collective-permute-start(bf16[1152,1,128]{0,2,1:T(8,128)(2,1)S(1)} %get-tuple-element.10), channel_id=1, source_target_pairs={{0,1},{1,2},{2,3},{3,4},{4,5},{5,6},{6,7},{8,9},{9,10},{10,11},{11... | collective-permute-start | bytes 884744 | tf_op jit(solution)/shard_map/ppermute | solution.py:21
  75.4 3.5 %collective-permute-start.1 = (bf16[1152,1,128]{0,2,1:T(8,128)(2,1)S(1)}, bf16[1152,1,128]{0,2,1:T(8,128)(2,1)S(1)}, u32[]{:S(2)}, u32[]{:S(2)}) collective-permute-start(bf16[1152,1,128]{0,2,1:T(8,128)(2,1)S(1)} %get-tuple-element.11), channel_id=1, source_target_pairs={{1,0},{2,1},{3,2},{4,3},{5,4},{6,5},{7,6},{9,8},{10,9},{11,10},{12... | collective-permute-start | bytes 884744 | tf_op jit(solution)/shard_map/ppermute | solution.py:22
  82.0 1.9 %copy-start.7 = (bf16[1152,1152]{1,0:T(8,128)(2,1)S(1)}, bf16[1152,1152]{1,0:T(8,128)(2,1)}, u32[]{:S(2)}) copy-start(bf16[1152,1152]{1,0:T(8,128)(2,1)} %param.13) | copy-start | bytes 7962628
where the time goes:
time: 147 us
  blocking collectives  57.5 us (39%)
  waiting for transfers between devices  31 us (21%)
  local copies, waits for them, and re-layouts  21 us (14%)
  matrix products  17.3 us (12%)
  other arithmetic  10.4 us (7%)
  starting transfers between devices  9.13 us (6%)
    all_to_all x1, blocking collectives, local(): lax.all_to_all(points, 'comp', split_axis=0, concat_axis=1, tiled=True)  36.7 us
    all_to_all x1, waiting for transfers between devices, local(): lax.all_to_all(advected, 'comp', split_axis=1, concat_axis=0, tiled=True)  29.2 us
    all_gather x2, blocking collectives, share_intersection(): everything = lax.all_gather(outgoing, 'grid', axis=0, tiled=True)  20.8 us
    dot_general x2, matrix products, source(): first_term = jnp.dot(coupling_a, points, preferred_element_type=jnp.float32)  7.29 us
    all_to_all x1, starting transfers between devices, local(): lax.all_to_all(advected, 'comp', split_axis=1, concat_axis=0, tiled=True)  6.35 us
    convert_element_type x2, local copies, waits for them, and re-layouts, propagate(): return values.reshape(count, -1).astype(jnp.bfloat16)  5.85 us
    dot_general x2, matrix products, source(): second = jnp.dot(coupling_b, points, preferred_element_type=jnp.float32)  5.19 us
    dot_general x2, matrix products, average(): lax.dot_general(weighted, onehot_table, (((0,), (0,)), ((), ())), preferr...  4.77 us
  transfers between devices with their start and end apart: 3, of which 2 were waited for; matrix products, arithmetic and copies ran while one was open for 0% of the time, Pallas kernels for 0%

commit v1 on v0

--- a/solution.py
+++ b/solution.py
@@ -1,8 +1,12 @@
+import functools
 import math
 
 import jax
 import jax.numpy as jnp
+import numpy as np
 from jax import lax
+from jax.experimental import pallas as pl
+from jax.experimental.pallas import tpu as pltpu
 from jax.sharding import PartitionSpec as P
 
 ND = 36
@@ -138,9 +142,475 @@
     return spectra[None]
 
 
+MESH = pl.DeviceIdType.MESH
+SUB = 16
+
+
+def coefficients(number):
+    square = number * number
+    return (1.0 - square, 0.5 * (square - number), 0.5 * (square + number))
+
+
+def flipped(index, mask, count):
+    total = 0
+    bit = 1
+    while bit < count:
+        total = total + lax.rem(index // bit + (mask // bit) % 2, 2) * bit
+        bit *= 2
+    return total
+
+
+def wave_kernel(
+    sizes,
+    spec_ref,
+    sea_ref,
+    cxy_ref,
+    a_hbm,
+    b_hbm,
+    send_ref,
+    recv_ref,
+    weight_ref,
+    out_ref,
+    a_ref,
+    b_ref,
+    table,
+    local_table,
+    outbox,
+    field,
+    updated,
+    averaged,
+    halo,
+    pick_table,
+    place_table,
+    inverse,
+    picked,
+    received,
+    scaled,
+    load_sem,
+    first_send,
+    first_recv,
+    share_send,
+    share_recv,
+    halo_send,
+    halo_recv,
+    last_send,
+    last_recv,
+):
+    pieces, groups, own, total, rows, slots = sizes
+    block_len = rows * LX
+    pairs = rows // 2
+    me = lax.axis_index("comp")
+    my_grid = lax.axis_index("grid")
+
+    load_a = pltpu.make_async_copy(a_hbm, a_ref, load_sem.at[0])
+    load_b = pltpu.make_async_copy(b_hbm, b_ref, load_sem.at[1])
+    load_a.start()
+    load_b.start()
+
+    barrier = pltpu.get_barrier_semaphore()
+    for mask in range(1, pieces):
+        pl.semaphore_signal(
+            barrier,
+            inc=1,
+            device_id={"comp": flipped(me, mask, pieces)},
+            device_id_type=MESH,
+        )
+    for shift in range(1, groups):
+        pl.semaphore_signal(
+            barrier,
+            inc=1,
+            device_id={"grid": lax.rem(my_grid + shift, groups)},
+            device_id_type=MESH,
+        )
+
+    lane = lax.broadcasted_iota(jnp.int32, (SUB, LX), 1)
+
+    def fill(source_row, target, target_row):
+        cx = jnp.broadcast_to(cxy_ref[pl.ds(source_row, SUB), 0:1], (SUB, LX))
+        cy = jnp.broadcast_to(cxy_ref[pl.ds(source_row, SUB), 1:2], (SUB, LX))
+        x0, xp, xm = coefficients(cx)
+        y0, yp, ym = coefficients(cy)
+        here = pl.ds(target_row, SUB)
+        target[0, here, :] = x0
+        target[1, here, :] = jnp.where(lane == LX - 1, 0.0, xp)
+        target[2, here, :] = jnp.where(lane == 0, 0.0, xm)
+        target[3, here, :] = y0
+        target[4, here, :] = yp
+        target[5, here, :] = ym
+
+    def fill_local(step, carry):
+        fill(
+            pl.multiple_of(me * own + step * SUB, SUB),
+            local_table,
+            pl.multiple_of(step * SUB, SUB),
+        )
+        return carry
+
+    lax.fori_loop(0, own // SUB, fill_local, 0)
+
+    def swept(value, sea, coefs):
+        return (
+            coefs[0] * value
+            + coefs[1] * pltpu.roll(value, LX - 1, 1)
+            + coefs[2] * pltpu.roll(value, 1, 1)
+        ) * sea
+
+    def crossed(middle, above, below, sea, coefs):
+        return ((coefs[3] * middle + coefs[4] * above + coefs[5] * below) * sea).astype(
+            jnp.bfloat16
+        )
+
+    lattice_rows = pieces * rows
+
+    def advect_first(peer, pair, store):
+        base = peer * rows + 2 * pair
+        where_rows = [
+            jnp.minimum(jnp.maximum(base - 1 + t, 0), lattice_rows - 1) for t in range(4)
+        ]
+        seas = [sea_ref[base + t] for t in range(4)]
+
+        def step(block, carry):
+            here = pl.ds(pl.multiple_of(block * SUB, SUB), SUB)
+            coefs = [local_table[i, here, :] for i in range(6)]
+            lines = [
+                swept(
+                    spec_ref[here, pl.ds(pl.multiple_of(row * LX, LX), LX)].astype(jnp.float32),
+                    seas[t],
+                    coefs,
+                )
+                for t, row in enumerate(where_rows)
+            ]
+            for t in range(2):
+                store(t, block, crossed(lines[t + 1], lines[t + 2], lines[t], seas[t + 1], coefs))
+            return carry
+
+        lax.fori_loop(0, own // SUB, step, 0)
+
+    order = list(range(pieces - 1, 0, -1))
+    mine = pl.ds(pl.multiple_of(me * own, SUB), own)
+
+    def first_copy(pair, mask):
+        return pltpu.make_async_remote_copy(
+            src_ref=outbox.at[pair, mask],
+            dst_ref=field.at[pl.ds(2 * pair, 2), mine, :],
+            send_sem=first_send.at[pair, mask],
+            recv_sem=first_recv.at[pair, mask],
+            device_id={"comp": flipped(me, mask, pieces)},
+            device_id_type=MESH,
+        )
+
+    for pair in range(pairs):
+        for mask in order:
+
+            def store_out(t, block, value, pair=pair, mask=mask):
+                here = pl.ds(pl.multiple_of(block * SUB, SUB), SUB)
+                outbox[pair, mask, t, here, :] = value
+
+            advect_first(flipped(me, mask, pieces), pair, store_out)
+            if pair == 0 and mask == order[0]:
+                pl.semaphore_wait(barrier, pieces - 1 + groups - 1)
+            first_copy(pair, mask).start()
+
+    for pair in range(pairs):
+
+        def store_own(t, block, value, pair=pair):
+            here = pl.ds(pl.multiple_of(me * own + block * SUB, SUB), SUB)
+            field[2 * pair + t, here, :] = value
+
+        advect_first(me, pair, store_own)
+
+    def fill_all(step, carry):
+        row = pl.multiple_of(step * SUB, SUB)
+        fill(row, table, row)
+        return carry
+
+    lax.fori_loop(0, total // SUB, fill_all, 0)
+
+    places = groups * slots
+    point = lax.broadcasted_iota(jnp.int32, (places, block_len), 1)
+    pick_table[...] = (send_ref[...] == point).astype(jnp.float32).astype(jnp.bfloat16)
+    hits = (recv_ref[...] == point).astype(jnp.float32)
+    place_table[...] = hits.astype(jnp.bfloat16)
+    inverse[...] = 1.0 / (1.0 + jnp.sum(hits * weight_ref[...], axis=0, keepdims=True))
+
+    @pl.when(me == 0)
+    def _():
+        halo[0] = jnp.zeros_like(halo[0])
+
+    @pl.when(me == pieces - 1)
+    def _():
+        halo[1] = jnp.zeros_like(halo[1])
+
+    load_a.wait()
+    load_b.wait()
+
+    tall = total // 3 if total % (3 * SUB) == 0 else total
+
+    def source_rows(one, two):
+        half = 0.5 * jnp.concatenate(
+            [sea_ref[me * rows + 1 + one], sea_ref[me * rows + 1 + two]], axis=1
+        )
+
+        def step(index, carry):
+            here = pl.ds(pl.multiple_of(index * tall, SUB), tall)
+            values = jnp.concatenate([field[one], field[two]], axis=1)
+            first = jnp.dot(a_ref[here, :], values, preferred_element_type=jnp.float32)
+            second = jnp.dot(b_ref[here, :], values, preferred_element_type=jnp.float32)
+            own_values = jnp.concatenate([field[one, here, :], field[two, here, :]], axis=1)
+            result = (own_values.astype(jnp.float32) + half * first * jnp.tanh(second)).astype(
+                jnp.bfloat16
+            )
+            updated[one, here, :] = result[:, :LX]
+            updated[two, here, :] = result[:, LX:]
+            return carry
+
+        lax.fori_loop(0, total // tall, step, 0)
+
+    def share_copy(turn, shift):
+        peer = lax.rem(my_grid + shift, groups)
+        return pltpu.make_async_remote_copy(
+            src_ref=picked.at[pl.ds(pl.multiple_of(peer * slots, SUB), slots), :],
+            dst_ref=received.at[turn, pl.ds(pl.multiple_of(my_grid * slots, SUB), slots), :],
+            send_sem=share_send.at[turn, shift],
+            recv_sem=share_recv.at[turn, shift],
+            device_id={"grid": peer},
+            device_id_type=MESH,
+        )
+
+    def share(turn):
+        everything = jnp.concatenate([updated[r] for r in range(rows)], axis=1)
+        chosen = lax.dot_general(
+            pick_table[...],
+            everything,
+            (((1,), (1,)), ((), ())),
+            preferred_element_type=jnp.float32,
+        )
+        picked[...] = chosen.astype(jnp.bfloat16)
+        for shift in range(1, groups):
+            share_copy(turn, shift).start()
+        here = pl.ds(pl.multiple_of(my_grid * slots, SUB), slots)
+        received[turn, here, :] = picked[here, :]
+        for shift in range(1, groups):
+            share_copy(turn, shift).wait()
+        scaled[...] = (
+            (received[turn].astype(jnp.float32) * weight_ref[...])
+            .astype(jnp.bfloat16)
+            .astype(jnp.float32)
+            .T.astype(jnp.bfloat16)
+        )
+
+    def average_rows(here, wanted):
+        for row in wanted:
+            columns = slice(row * LX, (row + 1) * LX)
+            added = jnp.dot(
+                scaled[here, :], place_table[:, columns], preferred_element_type=jnp.float32
+            )
+            averaged[row, here, :] = (
+                (updated[row, here, :].astype(jnp.float32) + added) * inverse[:, columns]
+            ).astype(jnp.bfloat16)
+
+    def halo_up():
+        return pltpu.make_async_remote_copy(
+            src_ref=averaged.at[rows - 1],
+            dst_ref=halo.at[0],
+            send_sem=halo_send.at[0],
+            recv_sem=halo_recv.at[0],
+            device_id={"comp": jnp.minimum(me + 1, pieces - 1)},
+            device_id_type=MESH,
+        )
+
+    def halo_down():
+        return pltpu.make_async_remote_copy(
+            src_ref=averaged.at[0],
+            dst_ref=halo.at[1],
+            send_sem=halo_send.at[1],
+            recv_sem=halo_recv.at[1],
+            device_id={"comp": jnp.maximum(me - 1, 0)},
+            device_id_type=MESH,
+        )
+
+    def advect_rows(wanted):
+        def step(block, carry):
+            here = pl.ds(pl.multiple_of(block * SUB, SUB), SUB)
+            coefs = [table[i, here, :] for i in range(6)]
+            lines = {}
+
+            def line(row):
+                if row not in lines:
+                    if row < 0:
+                        raw = halo[0, here, :]
+                    elif row >= rows:
+                        raw = halo[1, here, :]
+                    else:
+                        raw = averaged[row, here, :]
+                    lines[row] = swept(
+                        raw.astype(jnp.float32), sea_ref[me * rows + 1 + row], coefs
+                    )
+                return lines[row]
+
+            for row in wanted:
+                field[row, here, :] = crossed(
+                    line(row), line(row + 1), line(row - 1), sea_ref[me * rows + 1 + row], coefs
+                )
+            return carry
+
+        lax.fori_loop(0, total // SUB, step, 0)
+
+    for pair in range(pairs):
+        for mask in order:
+            first_copy(pair, mask).wait_recv()
+        source_rows(2 * pair, 2 * pair + 1)
+    for pair in range(pairs):
+        for mask in order:
+            first_copy(pair, mask).wait_send()
+
+    inner = list(range(1, rows - 1))
+    whole = pl.ds(0, total)
+    for turn in range(STEPS):
+        if turn > 0:
+
+            def average_step(index, carry, wanted):
+                average_rows(pl.ds(pl.multiple_of(index * own, SUB), own), wanted)
+                return carry
+
+            lax.fori_loop(
+                0, total // own, functools.partial(average_step, wanted=(0, rows - 1)), 0
+            )
+
+            @pl.when(me < pieces - 1)
+            def _():
+                halo_up().start()
+
+            @pl.when(me > 0)
+            def _():
+                halo_down().start()
+
+            lax.fori_loop(0, total // own, functools.partial(average_step, wanted=inner), 0)
+            advect_rows(inner)
+            for pair in range(len(inner) // 2):
+                source_rows(inner[2 * pair], inner[2 * pair + 1])
+
+            @pl.when(me < pieces - 1)
+            def _():
+                halo_up().wait_send()
+                halo_down().wait_recv()
+
+            @pl.when(me > 0)
+            def _():
+                halo_down().wait_send()
+                halo_up().wait_recv()
+
+            advect_rows((0, rows - 1))
+            source_rows(0, rows - 1)
+        share(turn)
+
+    def last_copy(mask):
+        peer = flipped(me, mask, pieces)
+        return pltpu.make_async_remote_copy(
+            src_ref=averaged.at[:, pl.ds(pl.multiple_of(peer * own, SUB), own), :],
+            dst_ref=out_ref.at[pl.ds(me * rows, rows)],
+            send_sem=last_send.at[mask],
+            recv_sem=last_recv.at[mask],
+            device_id={"comp": peer},
+            device_id_type=MESH,
+        )
+
+    for mask in order:
+        peer = flipped(me, mask, pieces)
+        average_rows(pl.ds(pl.multiple_of(peer * own, SUB), own), range(rows))
+        last_copy(mask).start()
+    average_rows(mine, range(rows))
+    for row in range(rows):
+        out_ref[me * rows + row] = averaged[row, mine, :]
+    for mask in order:
+        last_copy(mask).wait()
+
+
+def fused(spectrum, sea_mask, speed, coupling_a, coupling_b, send_index, recv_index, recv_weight):
+    own, columns = spectrum.shape[1:]
+    pieces = lax.axis_size("comp")
+    groups = lax.axis_size("grid")
+    total = coupling_a.shape[0]
+    rows = columns // pieces // LX
+    slots = send_index.shape[-1]
+    places = groups * slots
+    heading = (2.0 * math.pi / ND) * (np.arange(total) // NF)
+    turns = np.stack([np.cos(heading), np.sin(heading)], axis=1).astype(np.float32)
+    cxy = jnp.tile(speed[0], total // NF)[:, None] * jnp.asarray(turns)
+    sea = jnp.pad(sea_mask[0].astype(jnp.float32).reshape(-1, 1, LX), ((1, 1), (0, 0), (0, 0)))
+    vmem = pl.BlockSpec(memory_space=pltpu.VMEM)
+    anywhere = pl.BlockSpec(memory_space=pl.ANY)
+    half = jnp.bfloat16
+    dma = pltpu.SemaphoreType.DMA
+    lines = pl.pallas_call(
+        functools.partial(wave_kernel, (pieces, groups, own, total, rows, slots)),
+        out_shape=jax.ShapeDtypeStruct((pieces * rows, own, LX), half),
+        in_specs=[vmem, vmem, vmem, anywhere, anywhere, vmem, vmem, vmem],
+        out_specs=vmem,
+        scratch_shapes=[
+            pltpu.VMEM(coupling_a.shape, half),
+            pltpu.VMEM(coupling_b.shape, half),
+            pltpu.VMEM((6, total, LX), jnp.float32),
+            pltpu.VMEM((6, own, LX), jnp.float32),
+            pltpu.VMEM((rows // 2, pieces, 2, own, LX), half),
+            pltpu.VMEM((rows, total, LX), half),
+            pltpu.VMEM((rows, total, LX), half),
+            pltpu.VMEM((rows, total, LX), half),
+            pltpu.VMEM((2, total, LX), half),
+            pltpu.VMEM((places, rows * LX), half),
+            pltpu.VMEM((places, rows * LX), half),
+            pltpu.VMEM((1, rows * LX), jnp.float32),
+            pltpu.VMEM((places, total), half),
+            pltpu.VMEM((STEPS, places, total), half),
+            pltpu.VMEM((total, places), half),
+            dma((2,)),
+            dma((rows // 2, pieces)),
+            dma((rows // 2, pieces)),
+            dma((STEPS, groups)),
+            dma((STEPS, groups)),
+            dma((2,)),
+            dma((2,)),
+            dma((pieces,)),
+            dma((pieces,)),
+        ],
+        compiler_params=pltpu.CompilerParams(
+            collective_id=0, has_side_effects=True, vmem_limit_bytes=48 * 1024 * 1024
+        ),
+        name="wave_steps",
+    )(
+        spectrum[0],
+        sea,
+        cxy,
+        coupling_a,
+        coupling_b,
+        send_index.reshape(places, 1),
+        recv_index.reshape(places, 1),
+        recv_weight.reshape(places, 1),
+    )
+    return lines.transpose(1, 0, 2).reshape(1, own, columns)
+
+
+def fits(pieces, groups, own, rows, slots):
+    power = pieces & (pieces - 1) == 0
+    return power and own % SUB == 0 and rows % 2 == 0 and rows >= 4 and slots % SUB == 0
+
+
+def program(spectrum, sea_mask, speed, coupling_a, coupling_b, send_index, recv_index, recv_weight):
+    pieces = lax.axis_size("comp")
+    groups = lax.axis_size("grid")
+    rows = spectrum.shape[2] // pieces // LX
+    whole = rows * pieces * LX == spectrum.shape[2]
+    chosen = local
+    if whole and fits(pieces, groups, spectrum.shape[1], rows, send_index.shape[-1]):
+        chosen = fused
+    return chosen(
+        spectrum, sea_mask, speed, coupling_a, coupling_b, send_index, recv_index, recv_weight
+    )
+
+
 def solution(mesh):
     return jax.shard_map(
-        local,
+        program,
         mesh=mesh,
         in_specs=(
             P("grid", "comp", None),

time: 147 us -> 95.9 us (0.65)
  Pallas kernels: 0 us -> 87 us
  blocking collectives: 57.5 us -> 0 us
  waiting for transfers between devices: 31 us -> 0 us
  matrix products: 17.3 us -> 0 us
  local copies, waits for them, and re-layouts: 21 us -> 6.41 us
  starting transfers between devices: 9.13 us -> 0 us
  other arithmetic: 10.4 us -> 2.1 us
    pallas_call x0 -> x1, Pallas kernels: none -> 87 us  [fused(): pl.pallas_call(functools.partial(wave_kernel, (pieces, groups, own, total...]
    all_to_all x1 -> x0, blocking collectives: 36.7 us -> none  [local(): lax.all_to_all(points, 'comp', split_axis=0, concat_axis=1, tiled=True)]
    all_to_all x1 -> x0, waiting for transfers between devices: 29.2 us -> none  [local(): lax.all_to_all(advected, 'comp', split_axis=1, concat_axis=0, tiled=True)]
    all_gather x2 -> x0, blocking collectives: 20.8 us -> none  [share_intersection(): everything = lax.all_gather(outgoing, 'grid', axis=0, tiled=True)]
    dot_general x6 -> x0, matrix products: 17.3 us -> none  [the longest x2 7.29 us: source(): first_term = jnp.dot(coupling_a, points, preferred_element_type=jnp.float32)]
    convert_element_type x3 -> x0, local copies, waits for them, and re-layouts: 8.27 us -> none  [the longest x2 5.85 us: propagate(): return values.reshape(count, -1).astype(jnp.bfloat16)]
    all_to_all x1 -> x0, starting transfers between devices: 6.35 us -> none  [local(): lax.all_to_all(advected, 'comp', split_axis=1, concat_axis=0, tiled=True)]
    gather x2 -> x0, local copies, waits for them, and re-layouts: 4.51 us -> none  [share_intersection(): jnp.take(updated, targets, axis=1).T.reshape(groups, -1, total_comps)]
  transfers between devices with their start and end apart: 3 -> 0, of which waited for: 2 -> 0; matrix products, arithmetic and copies ran while one was open for 0% -> 0% of each run, Pallas kernels for 0% -> 0%
where the time goes in v1:
time: 95.9 us; the launch traced here: 95.6 us
  Pallas kernels  87 us (91%)
  local copies, waits for them, and re-layouts  6.41 us (7%)
  other arithmetic  2.1 us (2%)
    pallas_call x1, Pallas kernels, fused(): pl.pallas_call(functools.partial(wave_kernel, (pieces, groups, own, total...  87 us

profile of v1, /device:TPU:0, one launch (start us, length us, event | category | flops | bytes accessed | tf_op | source)
XLA Modules:
  0.0 95.6 jit_solution(17478608571067541590)
XLA Ops:
  0.0 0.0 copy-start.1
  0.0 0.8 convert_bitcast_fusion
  0.9 0.7 tile.8
  1.5 0.1 mul.10
  1.6 0.8 reshape.29.send_ref
  2.4 0.7 copy.19.recv_ref
  3.1 0.7 copy.20.weight_ref
  3.9 1.3 %broadcast_multiply_fusion.cxy_ref = f32[1152,2]{1,0:T(8,128)S(1)} fusion(f32[1152,2]{1,0:T(8,128)} %constant.5.clone, f32[1152]{0:T(1024)S(1)} %mul.10), kind=kLoop, calls=%fused_computation | loop fusion | flops 2304 | bytes 23040 | tf_op jit(solution)/shard_map/mul | solution.py:539
  5.1 0.0 copy-done.1
  5.1 0.0 copy-start
  5.2 1.7 %copy-done = bf16[1152,1152]{1,0:T(8,128)(2,1)S(1)} copy-done((bf16[1152,1152]{1,0:T(8,128)(2,1)S(1)}, bf16[1152,1152]{1,0:T(8,128)(2,1)}, u32[]{:S(2)}) %copy-start) | copy-done | bytes 2654232
  6.9 87.0 %wave_steps.1 = bf16[32,144,128]{2,1,0:T(8,128)(2,1)S(1)} custom-call(bf16[144,4096]{1,0:T(8,128)(2,1)S(1)} %bitcast.8, f32[34,1,128]{2,1,0:T(1,128)S(1)} %pad.4.sea_ref, f32[1152,2]{1,0:T(8,128)S(1)} %broadcast_multiply_fusion.cxy_ref, bf16[1152,1152]{1,0:T(8,128)(2,1)S(1)} %copy-done, bf16[1152,1152]{1,0:T(8,128)(2,1)} %b_hbm.1, ...), custom_call_target="tpu_custom_call" | custom-call | tf_op jit(solution)/shard_map/wave_steps/pallas_call | solution.py:545
  94.0 0.3 copy.21
  94.3 1.4 %reshape.28 = bf16[1,144,4096]{2,1,0:T(8,128)(2,1)} reshape(bf16[144,32,128]{2,1,0:T(8,128)(2,1)S(1)} %copy.21) | data formatting | bytes 2359296 | tf_op jit(solution)/shard_map/reshape | solution.py:590
  (1 shorter events, 0.0 us)
Async XLA Ops:
  0.0 5.1 %copy-start.1 = (bf16[1,144,4096]{2,1,0:T(8,128)(2,1)S(1)}, bf16[1,144,4096]{2,1,0:T(8,128)(2,1)}, u32[]{:S(2)}) copy-start(bf16[1,144,4096]{2,1,0:T(8,128)(2,1)} %param.9) | copy-start | bytes 3538948
  5.1 1.8 %copy-start = (bf16[1152,1152]{1,0:T(8,128)(2,1)S(1)}, bf16[1152,1152]{1,0:T(8,128)(2,1)}, u32[]{:S(2)}) copy-start(bf16[1152,1152]{1,0:T(8,128)(2,1)} %a_hbm.1) | copy-start | bytes 7962628

commit v2 on v1

--- a/solution.py
+++ b/solution.py
@@ -162,15 +162,18 @@
 
 def wave_kernel(
     sizes,
-    spec_ref,
+    spec_hbm,
     sea_ref,
-    cxy_ref,
+    speed_ref,
+    turn_ref,
     a_hbm,
     b_hbm,
     send_ref,
     recv_ref,
     weight_ref,
     out_ref,
+    spec_ref,
+    celerity,
     a_ref,
     b_ref,
     table,
@@ -179,10 +182,12 @@
     field,
     updated,
     averaged,
+    final,
     halo,
     pick_table,
     place_table,
     inverse,
+    weight,
     picked,
     received,
     scaled,
@@ -204,8 +209,8 @@
 
     load_a = pltpu.make_async_copy(a_hbm, a_ref, load_sem.at[0])
     load_b = pltpu.make_async_copy(b_hbm, b_ref, load_sem.at[1])
-    load_a.start()
-    load_b.start()
+    load_spec = pltpu.make_async_copy(spec_hbm, spec_ref, load_sem.at[2])
+    load_spec.start()
 
     barrier = pltpu.get_barrier_semaphore()
     for mask in range(1, pieces):
@@ -225,9 +230,20 @@
 
     lane = lax.broadcasted_iota(jnp.int32, (SUB, LX), 1)
 
+    def upright(row):
+        length = row.shape[1]
+        across = lax.broadcasted_iota(jnp.int32, (length, length), 1)
+        down = lax.broadcasted_iota(jnp.int32, (length, length), 0)
+        square = jnp.broadcast_to(row.astype(jnp.float32), (length, length))
+        return jnp.sum(jnp.where(across == down, square, 0.0), axis=1, keepdims=True)
+
+    celerity[...] = jnp.broadcast_to(upright(speed_ref[...]), celerity.shape)
+
     def fill(source_row, target, target_row):
-        cx = jnp.broadcast_to(cxy_ref[pl.ds(source_row, SUB), 0:1], (SUB, LX))
-        cy = jnp.broadcast_to(cxy_ref[pl.ds(source_row, SUB), 1:2], (SUB, LX))
+        part = pl.multiple_of(lax.rem(source_row, NF), SUB)
+        pace = celerity[pl.ds(part, SUB), :]
+        cx = pace * turn_ref[0, source_row // NF]
+        cy = pace * turn_ref[1, source_row // NF]
         x0, xp, xm = coefficients(cx)
         y0, yp, ym = coefficients(cy)
         here = pl.ds(target_row, SUB)
@@ -261,13 +277,21 @@
         )
 
     lattice_rows = pieces * rows
+    load_spec.wait()
+    load_a.start()
+    load_b.start()
+
+    def sea_line(row):
+        inside = jnp.minimum(jnp.maximum(row, 0), lattice_rows - 1)
+        line = sea_ref[:, pl.ds(pl.multiple_of(inside * LX, LX), LX)]
+        return jnp.where(inside == row, line, 0).astype(jnp.float32)
 
     def advect_first(peer, pair, store):
         base = peer * rows + 2 * pair
         where_rows = [
             jnp.minimum(jnp.maximum(base - 1 + t, 0), lattice_rows - 1) for t in range(4)
         ]
-        seas = [sea_ref[base + t] for t in range(4)]
+        seas = [sea_line(base - 1 + t) for t in range(4)]
 
         def step(block, carry):
             here = pl.ds(pl.multiple_of(block * SUB, SUB), SUB)
@@ -328,10 +352,16 @@
 
     places = groups * slots
     point = lax.broadcasted_iota(jnp.int32, (places, block_len), 1)
-    pick_table[...] = (send_ref[...] == point).astype(jnp.float32).astype(jnp.bfloat16)
-    hits = (recv_ref[...] == point).astype(jnp.float32)
+    spot = lax.broadcasted_iota(jnp.int32, (slots, block_len), 1).astype(jnp.float32)
+    for group in range(groups):
+        wanted = upright(send_ref[group : group + 1, :]) == spot
+        pick_table[group * slots : (group + 1) * slots, :] = wanted.astype(jnp.float32).astype(
+            jnp.bfloat16
+        )
+    hits = (upright(recv_ref[...]) == point.astype(jnp.float32)).astype(jnp.float32)
     place_table[...] = hits.astype(jnp.bfloat16)
-    inverse[...] = 1.0 / (1.0 + jnp.sum(hits * weight_ref[...], axis=0, keepdims=True))
+    weight[...] = upright(weight_ref[...])
+    inverse[...] = 1.0 / (1.0 + jnp.sum(hits * weight[...], axis=0, keepdims=True))
 
     @pl.when(me == 0)
     def _():
@@ -348,7 +378,7 @@
 
     def source_rows(one, two):
         half = 0.5 * jnp.concatenate(
-            [sea_ref[me * rows + 1 + one], sea_ref[me * rows + 1 + two]], axis=1
+            [sea_line(me * rows + one), sea_line(me * rows + two)], axis=1
         )
 
         def step(index, carry):
@@ -393,21 +423,20 @@
         for shift in range(1, groups):
             share_copy(turn, shift).wait()
         scaled[...] = (
-            (received[turn].astype(jnp.float32) * weight_ref[...])
+            (received[turn].astype(jnp.float32) * weight[...])
             .astype(jnp.bfloat16)
             .astype(jnp.float32)
             .T.astype(jnp.bfloat16)
         )
 
-    def average_rows(here, wanted):
+    def average_rows(here, wanted, store):
         for row in wanted:
             columns = slice(row * LX, (row + 1) * LX)
             added = jnp.dot(
                 scaled[here, :], place_table[:, columns], preferred_element_type=jnp.float32
             )
-            averaged[row, here, :] = (
-                (updated[row, here, :].astype(jnp.float32) + added) * inverse[:, columns]
-            ).astype(jnp.bfloat16)
+            value = (updated[row, here, :].astype(jnp.float32) + added) * inverse[:, columns]
+            store(row, value.astype(jnp.bfloat16))
 
     def halo_up():
         return pltpu.make_async_remote_copy(
@@ -430,6 +459,8 @@
         )
 
     def advect_rows(wanted):
+        seas = {row: sea_line(me * rows + row) for row in range(-1, rows + 1)}
+
         def step(block, carry):
             here = pl.ds(pl.multiple_of(block * SUB, SUB), SUB)
             coefs = [table[i, here, :] for i in range(6)]
@@ -443,14 +474,12 @@
                         raw = halo[1, here, :]
                     else:
                         raw = averaged[row, here, :]
-                    lines[row] = swept(
-                        raw.astype(jnp.float32), sea_ref[me * rows + 1 + row], coefs
-                    )
+                    lines[row] = swept(raw.astype(jnp.float32), seas[row], coefs)
                 return lines[row]
 
             for row in wanted:
                 field[row, here, :] = crossed(
-                    line(row), line(row + 1), line(row - 1), sea_ref[me * rows + 1 + row], coefs
+                    line(row), line(row + 1), line(row - 1), seas[row], coefs
                 )
             return carry
 
@@ -470,7 +499,12 @@
         if turn > 0:
 
             def average_step(index, carry, wanted):
-                average_rows(pl.ds(pl.multiple_of(index * own, SUB), own), wanted)
+                here = pl.ds(pl.multiple_of(index * own, SUB), own)
+
+                def store_row(row, value):
+                    averaged[row, here, :] = value
+
+                average_rows(here, wanted, store_row)
                 return carry
 
             lax.fori_loop(
@@ -504,11 +538,16 @@
             source_rows(0, rows - 1)
         share(turn)
 
+    def block_rows(peer):
+        return pl.ds(pl.multiple_of(peer * own, SUB), own)
+
+    my_points = pl.multiple_of(me * block_len, LX)
+
     def last_copy(mask):
         peer = flipped(me, mask, pieces)
         return pltpu.make_async_remote_copy(
-            src_ref=averaged.at[:, pl.ds(pl.multiple_of(peer * own, SUB), own), :],
-            dst_ref=out_ref.at[pl.ds(me * rows, rows)],
+            src_ref=final.at[block_rows(peer), :],
+            dst_ref=out_ref.at[:, pl.ds(my_points, block_len)],
             send_sem=last_send.at[mask],
             recv_sem=last_recv.at[mask],
             device_id={"comp": peer},
@@ -516,12 +555,18 @@
         )
 
     for mask in order:
-        peer = flipped(me, mask, pieces)
-        average_rows(pl.ds(pl.multiple_of(peer * own, SUB), own), range(rows))
+        here = block_rows(flipped(me, mask, pieces))
+
+        def store_final(row, value, here=here):
+            final[here, row * LX : (row + 1) * LX] = value
+
+        average_rows(here, range(rows), store_final)
         last_copy(mask).start()
-    average_rows(mine, range(rows))
-    for row in range(rows):
-        out_ref[me * rows + row] = averaged[row, mine, :]
+
+    def store_mine(row, value):
+        out_ref[:, pl.ds(pl.multiple_of(my_points + row * LX, LX), LX)] = value
+
+    average_rows(mine, range(rows), store_mine)
     for mask in order:
         last_copy(mask).wait()
 
@@ -534,20 +579,21 @@
     rows = columns // pieces // LX
     slots = send_index.shape[-1]
     places = groups * slots
-    heading = (2.0 * math.pi / ND) * (np.arange(total) // NF)
-    turns = np.stack([np.cos(heading), np.sin(heading)], axis=1).astype(np.float32)
-    cxy = jnp.tile(speed[0], total // NF)[:, None] * jnp.asarray(turns)
-    sea = jnp.pad(sea_mask[0].astype(jnp.float32).reshape(-1, 1, LX), ((1, 1), (0, 0), (0, 0)))
+    heading = (2.0 * math.pi / ND) * np.arange(total // NF)
+    turns = np.stack([np.cos(heading), np.sin(heading)]).astype(np.float32)
     vmem = pl.BlockSpec(memory_space=pltpu.VMEM)
-    anywhere = pl.BlockSpec(memory_space=pl.ANY)
+    anywhere = pl.BlockSpec(memory_space=pltpu.HBM)
     half = jnp.bfloat16
     dma = pltpu.SemaphoreType.DMA
+    smem = pl.BlockSpec(memory_space=pltpu.SMEM)
     lines = pl.pallas_call(
         functools.partial(wave_kernel, (pieces, groups, own, total, rows, slots)),
-        out_shape=jax.ShapeDtypeStruct((pieces * rows, own, LX), half),
-        in_specs=[vmem, vmem, vmem, anywhere, anywhere, vmem, vmem, vmem],
+        out_shape=jax.ShapeDtypeStruct((own, columns), half),
+        in_specs=[anywhere, vmem, vmem, smem, anywhere, anywhere, vmem, vmem, vmem],
         out_specs=vmem,
         scratch_shapes=[
+            pltpu.VMEM((own, columns), half),
+            pltpu.VMEM((NF, LX), jnp.float32),
             pltpu.VMEM(coupling_a.shape, half),
             pltpu.VMEM(coupling_b.shape, half),
             pltpu.VMEM((6, total, LX), jnp.float32),
@@ -556,14 +602,16 @@
             pltpu.VMEM((rows, total, LX), half),
             pltpu.VMEM((rows, total, LX), half),
             pltpu.VMEM((rows, total, LX), half),
+            pltpu.VMEM((total, rows * LX), half),
             pltpu.VMEM((2, total, LX), half),
             pltpu.VMEM((places, rows * LX), half),
             pltpu.VMEM((places, rows * LX), half),
             pltpu.VMEM((1, rows * LX), jnp.float32),
+            pltpu.VMEM((places, 1), jnp.float32),
             pltpu.VMEM((places, total), half),
             pltpu.VMEM((STEPS, places, total), half),
             pltpu.VMEM((total, places), half),
-            dma((2,)),
+            dma((3,)),
             dma((rows // 2, pieces)),
             dma((rows // 2, pieces)),
             dma((STEPS, groups)),
@@ -574,20 +622,21 @@
             dma((pieces,)),
         ],
         compiler_params=pltpu.CompilerParams(
-            collective_id=0, has_side_effects=True, vmem_limit_bytes=48 * 1024 * 1024
+            collective_id=0, has_side_effects=True, vmem_limit_bytes=64900000
         ),
         name="wave_steps",
     )(
         spectrum[0],
-        sea,
-        cxy,
+        sea_mask,
+        speed,
+        jnp.asarray(turns),
         coupling_a,
         coupling_b,
-        send_index.reshape(places, 1),
-        recv_index.reshape(places, 1),
-        recv_weight.reshape(places, 1),
-    )
-    return lines.transpose(1, 0, 2).reshape(1, own, columns)
+        send_index[0, 0],
+        recv_index[0],
+        recv_weight[0],
+    )
+    return lines[None]
 
 
 def fits(pieces, groups, own, rows, slots):

time: 95.9 us -> 91.3 us (0.952)
  local copies, waits for them, and re-layouts: 6.41 us -> 2.39 us
  other arithmetic: 2.1 us -> 0 us
  Pallas kernels: 87 us -> 88.7 us
    reshape x4 -> x0, local copies, waits for them, and re-layouts: 3.6 us -> none  [the longest x1 1.35 us: fused(): return lines.transpose(1, 0, 2).reshape(1, own, columns)]
    pallas_call x1, Pallas kernels: 87 us -> 88.7 us  [fused(): pl.pallas_call(functools.partial(wave_kernel, (pieces, groups, own, total...]
    mul x1 -> x0, other arithmetic: 1.28 us -> none  [fused(): cxy = jnp.tile(speed[0], total // NF)[:, None] * jnp.asarray(turns)]
    unnamed x4 -> x1, local copies, waits for them, and re-layouts: 1.75 us -> 2.39 us
where the time goes in v2:
time: 91.3 us; the launch traced here: 91.1 us
  Pallas kernels  88.7 us (97%)
  local copies, waits for them, and re-layouts  2.39 us (3%)
    pallas_call x1, Pallas kernels, fused(): pl.pallas_call(functools.partial(wave_kernel, (pieces, groups, own, total...  88.7 us
    unnamed x1, local copies, waits for them, and re-layouts  2.39 us

profile of v2, /device:TPU:0, one launch (start us, length us, event | category | flops | bytes accessed | tf_op | source)
XLA Modules:
  0.0 91.1 jit_solution(3818717828284681326)
XLA Ops:
  0.0 88.7 %wave_steps.1 = bf16[144,4096]{1,0:T(8,128)(2,1)} custom-call(bf16[144,4096]{1,0:T(8,128)(2,1)} %bitcast.6, s32[1,4096]{1,0:T(1,128)} %sea_ref.1, f32[1,32]{1,0:T(1,128)} %speed_ref.1, f32[2,36]{1,0:T(2,128)} %constant.2.clone.turn_ref, bf16[1152,1152]{1,0:T(8,128)(2,1)} %a_hbm.1, bf16[1152,1152]{1,0:T(8,128)(2,1)} %b_hbm.1, s32[4,16]{1,0:T(4,128)} %bitcast.7, ...), custom_call_target="tpu_custom_call" | custom-call | tf_op jit(solution)/shard_map/wave_steps/pallas_call | solution.py:589
  88.7 2.4 %copy.11 = bf16[1,144,4096]{2,1,0:T(8,128)(2,1)} copy(bf16[1,144,4096]{2,1,0:T(8,128)(2,1)} %bitcast.5) | data formatting | bytes 2359296

commit v3 on v2

--- a/solution.py
+++ b/solution.py
@@ -308,7 +308,7 @@
                 store(t, block, crossed(lines[t + 1], lines[t + 2], lines[t], seas[t + 1], coefs))
             return carry
 
-        lax.fori_loop(0, own // SUB, step, 0)
+        lax.fori_loop(0, own // SUB, step, 0, unroll=9)
 
     order = list(range(pieces - 1, 0, -1))
     mine = pl.ds(pl.multiple_of(me * own, SUB), own)
@@ -374,7 +374,7 @@
     load_a.wait()
     load_b.wait()
 
-    tall = total // 3 if total % (3 * SUB) == 0 else total
+    tall = total
 
     def source_rows(one, two):
         half = 0.5 * jnp.concatenate(
@@ -483,7 +483,7 @@
                 )
             return carry
 
-        lax.fori_loop(0, total // SUB, step, 0)
+        lax.fori_loop(0, total // SUB, step, 0, unroll=12)
 
     for pair in range(pairs):
         for mask in order:

time: 91.3 us -> 82.2 us (0.900)
  Pallas kernels: 88.7 us -> 79.6 us
    pallas_call x1, Pallas kernels: 88.7 us -> 79.6 us  [fused(): pl.pallas_call(functools.partial(wave_kernel, (pieces, groups, own, total...]
where the time goes in v3:
time: 82.2 us; the launch traced here: 81.9 us
  Pallas kernels  79.6 us (97%)
  local copies, waits for them, and re-layouts  2.39 us (3%)
    pallas_call x1, Pallas kernels, fused(): pl.pallas_call(functools.partial(wave_kernel, (pieces, groups, own, total...  79.6 us
    unnamed x1, local copies, waits for them, and re-layouts  2.39 us

profile of v3, /device:TPU:0, one launch (start us, length us, event | category | flops | bytes accessed | tf_op | source)
XLA Modules:
  0.0 81.9 jit_solution(1381734063898875225)
XLA Ops:
  0.0 79.6 %wave_steps.1 = bf16[144,4096]{1,0:T(8,128)(2,1)} custom-call(bf16[144,4096]{1,0:T(8,128)(2,1)} %bitcast.6, s32[1,4096]{1,0:T(1,128)} %sea_ref.1, f32[1,32]{1,0:T(1,128)} %speed_ref.1, f32[2,36]{1,0:T(2,128)} %constant.2.clone.turn_ref, bf16[1152,1152]{1,0:T(8,128)(2,1)} %a_hbm.1, bf16[1152,1152]{1,0:T(8,128)(2,1)} %b_hbm.1, s32[4,16]{1,0:T(4,128)} %bitcast.7, ...), custom_call_target="tpu_custom_call" | custom-call | tf_op jit(solution)/shard_map/wave_steps/pallas_call | solution.py:589
  79.6 2.4 %copy.11 = bf16[1,144,4096]{2,1,0:T(8,128)(2,1)} copy(bf16[1,144,4096]{2,1,0:T(8,128)(2,1)} %bitcast.5) | data formatting | bytes 2359296
